TPU v7x, 256 devices: a whole 4x4x8 slice. The times are simulated.
256 devices in a mesh: pts: 64 (over z, x, core), cen: 4 (over y).
Axes of the slice: x: 4, y: 4, z: 8, core: 2. Of those that a mesh axis runs over, the one named last changes fastest.
Arguments:
- points: bfloat16 [131072, 768], P('pts'), may hold values from -16 to 16
- centroids: bfloat16 [4096, 768], P('cen'), may hold values from -1 to 1
Outputs:
- new_centroids: bfloat16 [4096, 768], P(('cen', 'pts'))
- distances: float32 [131072], P('pts')
All inputs are finite; a program needn't handle non-finite values.
Results may differ from a plain program's by a relative error of at most 0.0034.
Values may be sent and summed in bfloat16 or wider, within the bound.
No kernel may reach another device: no remote copies, remote signals or barrier semaphores. Data moves between devices by JAX's collectives and lax.ppermute only.
A program may use at most 64 MiB of HBM per device.

v0:
```python
import math
import jax
import jax.numpy as jnp
from jax import lax
from jax.sharding import PartitionSpec as P

ITERS = 3
sharpness = 4.0


def merged(value, axis, join):
    pieces = jax.tree.map(lambda part: lax.all_gather(part, axis), value)
    head = jax.tree.map(lambda part: part[0], pieces)
    tail = jax.tree.map(lambda part: part[1:], pieces)
    subtotal, _ = lax.scan(lambda subtotal, piece: (join(subtotal, piece), None), head, tail)
    return subtotal


def logits(points, centroids):
    product = lax.dot_general(
        points, centroids, (((1,), (1,)), ((), ())), preferred_element_type=jnp.float32
    )
    return sharpness * product


def combine_lse(earlier, later):
    joined_max = jnp.maximum(earlier[0], later[0])
    summed = earlier[1] * jnp.exp(earlier[0] - joined_max) + later[1] * jnp.exp(
        later[0] - joined_max
    )
    return (joined_max, summed)


def on_device(points, centroids):
    pts_devices = lax.axis_size("pts")
    total_points = points.shape[0] * pts_devices
    local_centroids = centroids.shape[0]
    total_centroids = local_centroids * lax.axis_size("cen")
    width = points.shape[1]
    stored_scores = logits(points, centroids)

    def current_scores():
        return stored_scores

    col_potential = jnp.zeros((local_centroids,), jnp.float32)
    row_potential = jnp.zeros((points.shape[0],), jnp.float32)
    for iteration in range(ITERS):
        shifted = current_scores() + col_potential[None, :]
        highest = jnp.max(shifted, axis=1)
        summed = jnp.sum(jnp.exp(shifted - highest[:, None]), axis=1)
        highest, summed = merged((highest, summed), "cen", combine_lse)
        row_potential = -math.log(total_points) - (highest + jnp.log(summed))
        shifted = current_scores() + row_potential[:, None]
        highest = lax.pmax(jnp.max(shifted, axis=0), "pts")
        summed = lax.psum(jnp.sum(jnp.exp(shifted - highest[None, :]), axis=0), "pts")
        col_potential = -math.log(total_centroids) - (highest + jnp.log(summed))
    transport = jnp.exp(current_scores() + row_potential[:, None] + col_potential[None, :])
    weights = transport.astype(jnp.bfloat16)
    rows_each = local_centroids // pts_devices
    product = lax.dot_general(
        weights, points, (((0,), (0,)), ((), ())), preferred_element_type=jnp.float32
    )
    partial_sums = total_centroids * product
    gathered_block = lax.psum(partial_sums, "pts").astype(jnp.bfloat16)
    own_rows = lax.dynamic_slice_in_dim(
        gathered_block, lax.axis_index("pts") * rows_each, rows_each, 0
    )
    block_float = gathered_block.astype(jnp.float32)
    squares = jnp.sum(block_float * block_float, axis=1)
    cross_terms = lax.dot_general(
        points, gathered_block, (((1,), (1,)), ((), ())), preferred_element_type=jnp.float32
    )
    numerator = jnp.sum(transport * (squares[None, :] - 2.0 * cross_terms), axis=1)
    row_mass = jnp.sum(transport, axis=1)
    numerator, row_mass = lax.psum((numerator, row_mass), "cen")
    distances = numerator / row_mass / width
    return (own_rows, distances)


def solution(mesh):
    in_specs = (P("pts", None), P("cen", None))
    out_specs = (P(("cen", "pts"), None), P("pts"))
    return jax.shard_map(
        on_device, mesh=mesh, in_specs=in_specs, out_specs=out_specs, check_vma=False
    )
```

profile of v0, /device:TPU:0, one launch (start us, length us, event | category | flops | bytes accessed | tf_op | source)
XLA Modules:
  0.0 1194.2 jit_solution(11087072551796998977)
XLA Ops:
  0.6 0.0 copy-start
  0.6 1.9 copy-done
  2.5 7.0 fusion.10
  9.6 11.9 all-gather
  21.5 4.6 exponential_reduce_fusion.5
  26.0 11.9 all-gather.1
  38.0 0.2 while.36
  38.2 4.0 add_reduce_fusion.3
  42.2 125.5 %pmax.21 = f32[1024]{0:T(1024)S(1)} all-reduce(f32[1024]{0:T(1024)S(1)} %add_reduce_fusion.3), channel_id=1, replica_groups=mesh['pts'=64,'cen'=4] {'pts'}, use_global_device_ids=true, to_apply=%region_5.6 | all-reduce | flops 1024 | bytes 8192 | tf_op jit(solution)/shard_map/pmax | solution.py:54
  167.7 4.4 exponential_reduce_fusion.4
  172.1 124.4 %psum.42 = f32[1024]{0:T(1024)S(1)} all-reduce(f32[1024]{0:T(1024)S(1)} %exponential_reduce_fusion.4), channel_id=1, replica_groups=mesh['pts'=64,'cen'=4] {'pts'}, use_global_device_ids=true, to_apply=%region_7.8 | all-reduce | flops 1024 | bytes 8192 | tf_op jit(solution)/shard_map/psum | solution.py:55
  296.5 4.0 add_reduce_fusion.2
  300.5 11.9 all-gather.2
  312.4 4.3 exponential_reduce_fusion.3
  316.7 11.9 all-gather.3
  328.7 0.2 while.37
  328.9 4.0 add_reduce_fusion.1
  332.9 124.1 %pmax.22 = f32[1024]{0:T(1024)S(1)} all-reduce(f32[1024]{0:T(1024)S(1)} %add_reduce_fusion.1), channel_id=1, replica_groups=mesh['pts'=64,'cen'=4] {'pts'}, use_global_device_ids=true, to_apply=%region_13.14 | all-reduce | flops 1024 | bytes 8192 | tf_op jit(solution)/shard_map/pmax | solution.py:54
  457.0 4.4 exponential_reduce_fusion.2
  461.3 124.1 %psum.43 = f32[1024]{0:T(1024)S(1)} all-reduce(f32[1024]{0:T(1024)S(1)} %exponential_reduce_fusion.2), channel_id=1, replica_groups=mesh['pts'=64,'cen'=4] {'pts'}, use_global_device_ids=true, to_apply=%region_15.16 | all-reduce | flops 1024 | bytes 8192 | tf_op jit(solution)/shard_map/psum | solution.py:55
  585.4 4.0 add_reduce_fusion
  589.4 11.9 all-gather.4
  601.3 4.3 exponential_reduce_fusion.1
  605.6 11.9 all-gather.5
  617.6 0.2 while.38
  617.8 4.0 add_reduce_fusion.4
  621.8 124.1 %pmax.23 = f32[1024]{0:T(1024)S(1)} all-reduce(f32[1024]{0:T(1024)S(1)} %add_reduce_fusion.4), channel_id=1, replica_groups=mesh['pts'=64,'cen'=4] {'pts'}, use_global_device_ids=true, to_apply=%region_21.22 | all-reduce | flops 1024 | bytes 8192 | tf_op jit(solution)/shard_map/pmax | solution.py:54
  745.9 4.4 exponential_reduce_fusion
  750.3 124.2 %psum.44 = f32[1024]{0:T(1024)S(1)} all-reduce(f32[1024]{0:T(1024)S(1)} %exponential_reduce_fusion), channel_id=1, replica_groups=mesh['pts'=64,'cen'=4] {'pts'}, use_global_device_ids=true, to_apply=%region_23.24 | all-reduce | flops 1024 | bytes 8192 | tf_op jit(solution)/shard_map/psum | solution.py:55
  874.5 8.8 fusion.7
  883.3 279.3 %all-reduce.2 = bf16[1024,768]{1,0:T(8,128)(2,1)} all-reduce(f32[1024,768]{1,0:T(8,128)} %fusion.7), channel_id=1, replica_groups=mesh['pts'=64,'cen'=4] {'pts'}, use_global_device_ids=true, to_apply=%region_24.25 | all-reduce | flops 786432 | bytes 4718592 | tf_op jit(solution)/shard_map/psum | solution.py:64
  1162.6 1.3 constant_dynamic-slice_fusion.6
  1163.9 1.8 multiply_reduce_fusion
  1165.7 6.9 fusion
  1172.6 4.3 fusion.1
  1176.9 16.6 %all-reduce = (f32[2048]{0:T(1024)S(1)}, f32[2048]{0:T(1024)S(1)}) all-reduce(f32[2048]{0:T(1024)S(1)} %fusion, f32[2048]{0:T(1024)S(1)} %fusion.1), channel_id=1, replica_groups=mesh['pts'=64,'cen'=4] {'cen'}, use_global_device_ids=true, to_apply=%region_27.28 | all-reduce | flops 4096 | bytes 32768 | tf_op jit(solution)/shard_map/psum | solution.py:75
  1193.5 0.6 divide_multiply_fusion
  (42 shorter events, 0.5 us)
Async XLA Ops:
  0.6 1.9 copy-start
where the time goes:
time: 1190 us
  blocking collectives  1110 us (93%)
  other arithmetic  53.1 us (4%)
  matrix products  22.7 us (2%)
    pmax x3, blocking collectives, on_device(): highest = lax.pmax(jnp.max(shifted, axis=0), 'pts')  374 us
    psum x3, blocking collectives, on_device(): lax.psum(jnp.sum(jnp.exp(shifted - highest[None, :]), axis=0), 'pts')  373 us
    psum x1, blocking collectives, on_device(): gathered_block = lax.psum(partial_sums, 'pts').astype(jnp.bfloat16)  279 us
    all_gather x6, blocking collectives, merged(): pieces = jax.tree.map(lambda part: lax.all_gather(part, axis), value)  71.5 us

commit v1 on v0

--- a/solution.py
+++ b/solution.py
@@ -52,7 +52,9 @@
         row_potential = -math.log(total_points) - (highest + jnp.log(summed))
         shifted = current_scores() + row_potential[:, None]
         highest = lax.pmax(jnp.max(shifted, axis=0), "pts")
-        summed = lax.psum(jnp.sum(jnp.exp(shifted - highest[None, :]), axis=0), "pts")
+        own = jnp.sum(jnp.exp(shifted - highest[None, :]), axis=0)
+        parts = lax.all_gather(own, "pts")
+        summed = jnp.sum(parts, axis=0)
         col_potential = -math.log(total_centroids) - (highest + jnp.log(summed))
     transport = jnp.exp(current_scores() + row_potential[:, None] + col_potential[None, :])
     weights = transport.astype(jnp.bfloat16)

time: 1190 us -> 957 us (0.80)
  blocking collectives: 1110 us -> 871 us
    psum x3 -> x0, blocking collectives: 373 us -> none  [on_device(): lax.psum(jnp.sum(jnp.exp(shifted - highest[None, :]), axis=0), 'pts')]
    all_gather x0 -> x3, blocking collectives: none -> 126 us  [on_device(): parts = lax.all_gather(own, 'pts')]
where the time goes in v1:
time: 957 us; the launch traced here: 956 us
  blocking collectives  871 us (91%)
  other arithmetic  55.1 us (6%)
  matrix products  22.7 us (2%)
    pmax x3, blocking collectives, on_device(): highest = lax.pmax(jnp.max(shifted, axis=0), 'pts')  374 us
    psum x1, blocking collectives, on_device(): gathered_block = lax.psum(partial_sums, 'pts').astype(jnp.bfloat16)  283 us
    all_gather x3, blocking collectives, on_device(): parts = lax.all_gather(own, 'pts')  126 us
    all_gather x6, blocking collectives, merged(): pieces = jax.tree.map(lambda part: lax.all_gather(part, axis), value)  71.5 us

profile of v1, /device:TPU:0, one launch (start us, length us, event | category | flops | bytes accessed | tf_op | source)
XLA Modules:
  0.0 955.7 jit_solution(653687739994679006)
XLA Ops:
  0.6 0.0 copy-start
  0.6 1.9 copy-done
  2.5 7.0 fusion.10
  9.6 11.9 %all-gather = f32[8192]{0:T(1024)S(1)} all-gather(f32[2048]{0:T(1024)S(1)} %get-tuple-element.136), channel_id=2, replica_groups=mesh['pts'=64,'cen'=4] {'cen'}, dimensions={0}, use_global_device_ids=true | all-gather | bytes 40960 | tf_op jit(solution)/shard_map/all_gather | solution.py:12
  21.5 4.6 exponential_reduce_fusion.5
  26.0 11.9 %all-gather.1 = f32[8192]{0:T(1024)S(1)} all-gather(f32[2048]{0:T(1024)S(1)} %exponential_reduce_fusion.5), channel_id=3, replica_groups=mesh['pts'=64,'cen'=4] {'cen'}, dimensions={0}, use_global_device_ids=true | all-gather | bytes 40960 | tf_op jit(solution)/shard_map/all_gather | solution.py:12
  38.0 0.2 while.36
  38.2 4.0 add_reduce_fusion.3
  42.2 125.5 %pmax.21 = f32[1024]{0:T(1024)S(1)} all-reduce(f32[1024]{0:T(1024)S(1)} %add_reduce_fusion.3), channel_id=1, replica_groups=mesh['pts'=64,'cen'=4] {'pts'}, use_global_device_ids=true, to_apply=%region_5.6 | all-reduce | flops 1024 | bytes 8192 | tf_op jit(solution)/shard_map/pmax | solution.py:54
  167.7 4.4 exponential_reduce_fusion.4
  172.1 41.0 %all-gather.2 = f32[65536]{0:T(1024)S(1)} all-gather(f32[1024]{0:T(1024)S(1)} %exponential_reduce_fusion.4), channel_id=4, replica_groups=mesh['pts'=64,'cen'=4] {'pts'}, dimensions={0}, use_global_device_ids=true | all-gather | bytes 266240 | tf_op jit(solution)/shard_map/all_gather | solution.py:56
  213.1 0.8 reshape.19
  213.8 1.0 reduce_sum.110
  214.8 4.0 add_reduce_fusion.2
  218.8 11.9 %all-gather.3 = f32[8192]{0:T(1024)S(1)} all-gather(f32[2048]{0:T(1024)S(1)} %add_reduce_fusion.2), channel_id=5, replica_groups=mesh['pts'=64,'cen'=4] {'cen'}, dimensions={0}, use_global_device_ids=true | all-gather | bytes 40960 | tf_op jit(solution)/shard_map/all_gather | solution.py:12
  230.7 4.3 exponential_reduce_fusion.3
  235.1 11.9 %all-gather.4 = f32[8192]{0:T(1024)S(1)} all-gather(f32[2048]{0:T(1024)S(1)} %exponential_reduce_fusion.3), channel_id=6, replica_groups=mesh['pts'=64,'cen'=4] {'cen'}, dimensions={0}, use_global_device_ids=true | all-gather | bytes 40960 | tf_op jit(solution)/shard_map/all_gather | solution.py:12
  247.0 0.2 while.37
  247.2 4.0 add_reduce_fusion.1
  251.2 124.1 %pmax.22 = f32[1024]{0:T(1024)S(1)} all-reduce(f32[1024]{0:T(1024)S(1)} %add_reduce_fusion.1), channel_id=1, replica_groups=mesh['pts'=64,'cen'=4] {'pts'}, use_global_device_ids=true, to_apply=%region_13.14 | all-reduce | flops 1024 | bytes 8192 | tf_op jit(solution)/shard_map/pmax | solution.py:54
  375.3 4.4 exponential_reduce_fusion.2
  379.7 41.2 %all-gather.5 = f32[65536]{0:T(1024)S(1)} all-gather(f32[1024]{0:T(1024)S(1)} %exponential_reduce_fusion.2), channel_id=7, replica_groups=mesh['pts'=64,'cen'=4] {'pts'}, dimensions={0}, use_global_device_ids=true | all-gather | bytes 266240 | tf_op jit(solution)/shard_map/all_gather | solution.py:56
  420.8 0.8 reshape.22
  421.6 1.0 reduce_sum.113
  422.6 4.0 add_reduce_fusion
  426.6 11.9 %all-gather.6 = f32[8192]{0:T(1024)S(1)} all-gather(f32[2048]{0:T(1024)S(1)} %add_reduce_fusion), channel_id=8, replica_groups=mesh['pts'=64,'cen'=4] {'cen'}, dimensions={0}, use_global_device_ids=true | all-gather | bytes 40960 | tf_op jit(solution)/shard_map/all_gather | solution.py:12
  438.5 4.3 exponential_reduce_fusion.1
  442.8 11.9 %all-gather.7 = f32[8192]{0:T(1024)S(1)} all-gather(f32[2048]{0:T(1024)S(1)} %exponential_reduce_fusion.1), channel_id=9, replica_groups=mesh['pts'=64,'cen'=4] {'cen'}, dimensions={0}, use_global_device_ids=true | all-gather | bytes 40960 | tf_op jit(solution)/shard_map/all_gather | solution.py:12
  454.8 0.2 while.38
  455.0 4.0 add_reduce_fusion.4
  459.0 124.1 %pmax.23 = f32[1024]{0:T(1024)S(1)} all-reduce(f32[1024]{0:T(1024)S(1)} %add_reduce_fusion.4), channel_id=1, replica_groups=mesh['pts'=64,'cen'=4] {'pts'}, use_global_device_ids=true, to_apply=%region_21.22 | all-reduce | flops 1024 | bytes 8192 | tf_op jit(solution)/shard_map/pmax | solution.py:54
  583.1 4.4 exponential_reduce_fusion
  587.4 44.3 %all-gather.8 = f32[65536]{0:T(1024)} all-gather(f32[1024]{0:T(1024)S(1)} %exponential_reduce_fusion), channel_id=10, replica_groups=mesh['pts'=64,'cen'=4] {'pts'}, dimensions={0}, use_global_device_ids=true | all-gather | bytes 266240 | tf_op jit(solution)/shard_map/all_gather | solution.py:56
  631.7 1.0 reshape.25
  632.8 8.8 fusion.7
  641.6 282.5 %all-reduce.2 = bf16[1024,768]{1,0:T(8,128)(2,1)} all-reduce(f32[1024,768]{1,0:T(8,128)} %fusion.7), channel_id=1, replica_groups=mesh['pts'=64,'cen'=4] {'pts'}, use_global_device_ids=true, to_apply=%region_24.25 | all-reduce | flops 786432 | bytes 4718592 | tf_op jit(solution)/shard_map/psum | solution.py:66
  924.1 1.3 constant_dynamic-slice_fusion.6
  925.4 1.8 multiply_reduce_fusion
  927.2 6.9 fusion
  934.1 4.3 fusion.1
  938.4 16.6 %all-reduce = (f32[2048]{0:T(1024)S(1)}, f32[2048]{0:T(1024)S(1)}) all-reduce(f32[2048]{0:T(1024)S(1)} %fusion, f32[2048]{0:T(1024)S(1)} %fusion.1), channel_id=1, replica_groups=mesh['pts'=64,'cen'=4] {'cen'}, use_global_device_ids=true, to_apply=%region_27.28 | all-reduce | flops 4096 | bytes 32768 | tf_op jit(solution)/shard_map/psum | solution.py:77
  955.1 0.6 divide_multiply_fusion
  (43 shorter events, 0.5 us)
Async XLA Ops:
  0.6 1.9 copy-start
